TPU v7x, 32 devices: a whole 2x2x4 slice. The times are simulated.
32 devices in a mesh: grp: 4 (over y, x), tp: 8 (over z, core).
Axes of the slice: x: 2, y: 2, z: 4, core: 2. Of those that a mesh axis runs over, the one named last changes fastest.
Arguments:
- batch_sizes: int32 [4], P('grp'), may hold values from 1 to 16
- seq_lens: int32 [4, 16], P('grp'), may hold values from 1 to 2048
- page_table: int32 [4, 16, 128], P('grp', None, 'tp'), may hold values from 0 to 255, as said below
- queries: bfloat16 [4, 16, 4096], P('grp', None, 'tp'), may hold values from -4 to 14
- kv_pool: bfloat16 [4, 2048, 16, 1024], P('grp', 'tp'), may hold values from -7 to 7
- new_kv: bfloat16 [4, 16, 1024], P('grp'), may hold values from -6 to 6
- out_weight: bfloat16 [4096, 2880], P('tp', 'grp'), may hold values from -0.375 to 0.375
Outputs:
- mixed: float32 [4, 16, 2880], P('grp')
Inputs may be any that keep to these rules, and one draw needn't show every extreme that they name: `batch_sizes`: slots below a group's batch size are live; the others are empty and their outputs are zero. `seq_lens`: entries of empty slots are drawn but unused. `page_table`: for every group g and every t, the entries [g, :, t * 16 to (t + 1) * 16 - 1] are a permutation of 0 to 255.
All inputs are finite; a program needn't handle non-finite values.
Results may differ from a plain program's by a relative error of at most 0.007.
Values may be sent and summed in bfloat16 or wider, within the bound.
A program may use at most 64 MiB of HBM per device.

v0:
```python
import jax
import jax.numpy as jnp
from jax import lax
from jax.sharding import PartitionSpec as P

HEADS = 64
KV_HEADS = 8
HD = 64
SLOT_BLOCK = 2
PRECISE = lax.Precision.HIGHEST
NEG_BIG = -1e30


def attend_slots(query_rows, page_blocks, lengths, tp_index, tp_count, kv_heads):
    slot_count, page_count, page_len, row_width = page_blocks.shape
    head_dim = row_width // (2 * kv_heads)
    head_count = query_rows.shape[1] // head_dim
    group_size = head_count // kv_heads
    token_count = page_count * page_len
    token_rows = page_blocks.reshape(slot_count, token_count, row_width)
    key_rows = token_rows[:, :, : row_width // 2].reshape(
        slot_count, token_count, kv_heads, head_dim
    )
    value_rows = token_rows[:, :, row_width // 2 :].reshape(
        slot_count, token_count, kv_heads, head_dim
    )
    grouped = query_rows.reshape(slot_count, kv_heads, group_size, head_dim)
    scores = jnp.einsum("skgd,stkd->skgt", grouped, key_rows, preferred_element_type=jnp.float32)
    scores = scores * head_dim ** (-0.5)
    page_index = lax.broadcasted_iota(jnp.int32, (page_count, page_len), 0)
    token_index = lax.broadcasted_iota(jnp.int32, (page_count, page_len), 1)
    position = ((page_index * tp_count + tp_index) * page_len + token_index).reshape(token_count)
    valid_mask = (position[None, :] < lengths[:, None])[:, None, None, :]
    scores = jnp.where(valid_mask, scores, NEG_BIG)
    top_score = jnp.max(scores, axis=3)
    weights = jnp.where(valid_mask, jnp.exp(scores - top_score[..., None]), 0.0)
    weight_sum = jnp.sum(weights, axis=3)
    weighted = jnp.einsum(
        "skgt,stkd->skgd",
        weights.astype(jnp.bfloat16),
        value_rows,
        preferred_element_type=jnp.float32,
    )
    return (
        weighted.reshape(slot_count, head_count * head_dim),
        top_score.reshape(slot_count, head_count),
        weight_sum.reshape(slot_count, head_count),
    )


def local(batch_sizes, seq_lens, page_table, queries, kv_pool, new_kv, out_weight):
    tp_count = lax.axis_size("tp")
    tp_index = lax.axis_index("tp")
    gathered = lax.all_gather(queries, "tp", axis=2, tiled=True)[0]
    kv_pages = kv_pool[0]
    page_ids = page_table[0]
    lengths = seq_lens[0]
    live_count = batch_sizes[0]
    slot_count, full_width = gathered.shape
    head_dim = HD
    head_count = HEADS
    slot_order = jnp.arange(slot_count, dtype=jnp.int32)

    def local_block(block_index, state):
        first_slot = block_index * SLOT_BLOCK
        query_rows = lax.dynamic_slice_in_dim(gathered, first_slot, SLOT_BLOCK, 0)
        block_ids = lax.dynamic_slice_in_dim(page_ids, first_slot, SLOT_BLOCK, 0)
        block_lengths = lax.dynamic_slice_in_dim(lengths, first_slot, SLOT_BLOCK, 0)
        block_slots = first_slot + jnp.arange(SLOT_BLOCK, dtype=jnp.int32)
        block_lengths = jnp.where(block_slots < live_count, block_lengths, 0)
        pieces = attend_slots(
            query_rows, kv_pages[block_ids], block_lengths, tp_index, tp_count, KV_HEADS
        )
        return tuple(
            (
                lax.dynamic_update_slice_in_dim(whole, piece, first_slot, 0)
                for whole, piece in zip(state, pieces)
            )
        )

    start_state = (
        jnp.zeros((slot_count, full_width), jnp.float32),
        jnp.full((slot_count, head_count), NEG_BIG, jnp.float32),
        jnp.zeros((slot_count, head_count), jnp.float32),
    )
    block_total = (live_count + SLOT_BLOCK - 1) // SLOT_BLOCK
    weighted, top_score, weight_sum = lax.fori_loop(0, block_total, local_block, start_state)
    own_heads = head_count // tp_count
    own_width = own_heads * head_dim
    shard_weighted, shard_top, shard_sum = (
        lax.all_to_all(weighted[None], "tp", split_axis=2, concat_axis=0, tiled=True),
        lax.all_to_all(top_score[None], "tp", split_axis=2, concat_axis=0, tiled=True),
        lax.all_to_all(weight_sum[None], "tp", split_axis=2, concat_axis=0, tiled=True),
    )
    part_top = jnp.max(shard_top, axis=0)
    shard_rescale = jnp.exp(shard_top - part_top[None])
    part_weighted = jnp.sum(shard_weighted * jnp.repeat(shard_rescale, head_dim, axis=-1), axis=0)
    part_sum = jnp.sum(shard_sum * shard_rescale, axis=0)
    fresh_rows = new_kv[0].astype(jnp.float32)
    kv_width = KV_HEADS * head_dim
    new_keys = fresh_rows[:, :kv_width].reshape(slot_count, KV_HEADS, head_dim)
    new_values = fresh_rows[:, kv_width:].reshape(slot_count, KV_HEADS, head_dim)
    head_ids = tp_index * own_heads + jnp.arange(own_heads, dtype=jnp.int32)
    head_map = (
        head_ids[:, None] // (head_count // KV_HEADS)
        == jnp.arange(KV_HEADS, dtype=jnp.int32)[None, :]
    ).astype(jnp.float32)
    own_keys = jnp.einsum("jk,skd->sjd", head_map, new_keys, precision=PRECISE)
    own_values = jnp.einsum("jk,skd->sjd", head_map, new_values, precision=PRECISE)
    own_queries = queries[0].astype(jnp.float32).reshape(slot_count, own_heads, head_dim)
    self_score = jnp.sum(own_queries * own_keys, axis=-1) * head_dim ** (-0.5)
    final_top = jnp.maximum(part_top, self_score)
    cache_rescale = jnp.exp(part_top - final_top)
    self_rescale = jnp.exp(self_score - final_top)
    numerator = part_weighted.reshape(slot_count, own_heads, head_dim) * cache_rescale[..., None]
    numerator = numerator + own_values * self_rescale[..., None]
    denominator = part_sum * cache_rescale + self_rescale
    attended = (numerator / denominator[..., None]).reshape(slot_count, own_width)
    attended = jnp.where((slot_order < live_count)[:, None], attended, 0.0).astype(jnp.bfloat16)
    projected = jnp.dot(
        attended,
        lax.all_gather(out_weight, "grp", axis=1, tiled=True),
        preferred_element_type=jnp.float32,
    )
    mixed = lax.psum(projected, "tp")
    return mixed[None]


def solution(mesh):
    return jax.shard_map(
        local,
        mesh=mesh,
        in_specs=(
            P("grp"),
            P("grp", None),
            P("grp", None, "tp"),
            P("grp", None, "tp"),
            P("grp", "tp", None, None),
            P("grp", None, None),
            P("tp", "grp"),
        ),
        out_specs=P("grp", None, None),
        check_vma=False,
    )
```

profile of v0, /device:TPU:0, one launch (start us, length us, event | category | flops | bytes accessed | tf_op | source)
XLA Modules:
  0.0 214.4 jit_solution(14500293375372935720)
XLA Ops:
  6.5 0.7 all-gather.2.cloned.1.call-update
  7.9 15.9 %all_gather.6 = bf16[1,16,4096]{2,1,0:T(8,128)(2,1)S(1)} all-gather(bf16[1,16,512]{2,1,0:T(8,128)(2,1)} %param.12), channel_id=1, replica_groups=mesh['grp'=4,'tp'=8] {'tp'}, dimensions={2}, use_global_device_ids=true | all-gather | bytes 147456 | tf_op jit(solution)/shard_map/all_gather | solution.py:54
  23.9 65.7 %while.14 = (s32[]{:T(128)}, f32[16,4096]{1,0:T(8,128)S(1)}, f32[16,64]{1,0:T(8,128)S(1)}, f32[16,64]{1,0:T(8,128)S(1)}, s32[]{:T(128)}, /*index=5*/s32[]{:T(128...) while((s32[]{:T(128)}, f32[16,4096]{1,0:T(8,128)S(1)}, ...), condition=%wide.region_3.4_spmd, body=%wide.region_0.3_spmd.sunk | while | flops 8685212 | bytes 7998579 | solution.py:87
  24.0 1.4 compare_select_fusion.8
  25.6 0.7 compare_select_fusion.7
  26.4 4.0 %gather_fusion = bf16[32,16,1024]{2,1,0:T(8,128)(2,1)S(1)} fusion(bf16[256,16,1024]{2,1,0:T(8,128)(2,1)} %get-tuple-element.223, s32[1024]{0:T(1024)S(1)} %pad_clamp_fusion.2), kind=kCustom, calls=%fused_computation.clone.1 | custom fusion | bytes 2097280 | tf_op jit(solution)/shard_map/while/body/gather | solution.py:72
  30.8 0.3 fusion.49
  31.6 0.3 fusion.50
  32.1 1.4 compare_select_fusion.8
  33.7 0.7 compare_select_fusion.7
  34.5 4.5 %gather_fusion = bf16[32,16,1024]{2,1,0:T(8,128)(2,1)S(1)} fusion(bf16[256,16,1024]{2,1,0:T(8,128)(2,1)} %get-tuple-element.223, s32[1024]{0:T(1024)S(1)} %pad_clamp_fusion.2), kind=kCustom, calls=%fused_computation.clone.1 | custom fusion | bytes 2097280 | tf_op jit(solution)/shard_map/while/body/gather | solution.py:72
  39.5 0.3 fusion.49
  40.3 0.3 fusion.50
  40.8 1.4 compare_select_fusion.8
  42.4 0.7 compare_select_fusion.7
  43.2 4.0 %gather_fusion = bf16[32,16,1024]{2,1,0:T(8,128)(2,1)S(1)} fusion(bf16[256,16,1024]{2,1,0:T(8,128)(2,1)} %get-tuple-element.223, s32[1024]{0:T(1024)S(1)} %pad_clamp_fusion.2), kind=kCustom, calls=%fused_computation.clone.1 | custom fusion | bytes 2097280 | tf_op jit(solution)/shard_map/while/body/gather | solution.py:72
  47.6 0.3 fusion.49
  48.4 0.3 fusion.50
  48.9 1.4 compare_select_fusion.8
  50.5 0.7 compare_select_fusion.7
  51.3 4.0 %gather_fusion = bf16[32,16,1024]{2,1,0:T(8,128)(2,1)S(1)} fusion(bf16[256,16,1024]{2,1,0:T(8,128)(2,1)} %get-tuple-element.223, s32[1024]{0:T(1024)S(1)} %pad_clamp_fusion.2), kind=kCustom, calls=%fused_computation.clone.1 | custom fusion | bytes 2097280 | tf_op jit(solution)/shard_map/while/body/gather | solution.py:72
  55.7 0.3 fusion.49
  56.6 0.3 fusion.50
  57.0 1.4 compare_select_fusion.8
  58.7 0.7 compare_select_fusion.7
  59.5 4.0 %gather_fusion = bf16[32,16,1024]{2,1,0:T(8,128)(2,1)S(1)} fusion(bf16[256,16,1024]{2,1,0:T(8,128)(2,1)} %get-tuple-element.223, s32[1024]{0:T(1024)S(1)} %pad_clamp_fusion.2), kind=kCustom, calls=%fused_computation.clone.1 | custom fusion | bytes 2097280 | tf_op jit(solution)/shard_map/while/body/gather | solution.py:72
  63.9 0.3 fusion.49
  64.7 0.3 fusion.50
  65.2 1.4 compare_select_fusion.8
  66.8 0.7 compare_select_fusion.7
  67.6 4.0 %gather_fusion = bf16[32,16,1024]{2,1,0:T(8,128)(2,1)S(1)} fusion(bf16[256,16,1024]{2,1,0:T(8,128)(2,1)} %get-tuple-element.223, s32[1024]{0:T(1024)S(1)} %pad_clamp_fusion.2), kind=kCustom, calls=%fused_computation.clone.1 | custom fusion | bytes 2097280 | tf_op jit(solution)/shard_map/while/body/gather | solution.py:72
  72.0 0.3 fusion.49
  72.9 0.3 fusion.50
  73.3 1.4 compare_select_fusion.8
  75.0 0.7 compare_select_fusion.7
  75.7 4.0 %gather_fusion = bf16[32,16,1024]{2,1,0:T(8,128)(2,1)S(1)} fusion(bf16[256,16,1024]{2,1,0:T(8,128)(2,1)} %get-tuple-element.223, s32[1024]{0:T(1024)S(1)} %pad_clamp_fusion.2), kind=kCustom, calls=%fused_computation.clone.1 | custom fusion | bytes 2097280 | tf_op jit(solution)/shard_map/while/body/gather | solution.py:72
  80.2 0.3 fusion.49
  81.0 0.3 fusion.50
  81.5 1.4 compare_select_fusion.8
  83.1 0.7 compare_select_fusion.7
  83.9 4.0 %gather_fusion = bf16[32,16,1024]{2,1,0:T(8,128)(2,1)S(1)} fusion(bf16[256,16,1024]{2,1,0:T(8,128)(2,1)} %get-tuple-element.223, s32[1024]{0:T(1024)S(1)} %pad_clamp_fusion.2), kind=kCustom, calls=%fused_computation.clone.1 | custom fusion | bytes 2097280 | tf_op jit(solution)/shard_map/while/body/gather | solution.py:72
  88.3 0.3 fusion.49
  89.2 0.3 fusion.50
  89.7 0.5 broadcast.132
  90.2 0.7 reduce.5
  90.9 0.7 reshape.169
  91.6 4.6 %all-to-all-start.1 = ((f32[8,1,128]{2,1,0:T(1,128)}), f32[8,1,128]{2,1,0:T(1,128)S(1)}, u32[]{:S(2)}, u32[]{:S(2)}) async-start(f32[8,1,128]{2,1,0:T(1,128)} %reshape.169), calls=%async_computation.1 | async-start | bytes 8192 | tf_op jit(solution)/shard_map/all_to_all | solution.py:92
  96.4 0.7 reduce.3
  97.1 0.7 reshape.171
  97.9 3.9 %all-to-all-done.1 = f32[8,1,128]{2,1,0:T(1,128)S(1)} async-done(((f32[8,1,128]{2,1,0:T(1,128)}), f32[8,1,128]{2,1,0:T(1,128)S(1)}, u32[]{:S(2)}, u32[]{:S(2)}) %all-to-all-start.1) | async-done | bytes 4128 | tf_op jit(solution)/shard_map/all_to_all | solution.py:92
  101.8 3.3 %all-to-all-start.2 = ((f32[8,1,128]{2,1,0:T(1,128)}), f32[8,1,128]{2,1,0:T(1,128)S(1)}, u32[]{:S(2)}, u32[]{:S(2)}) async-start(f32[8,1,128]{2,1,0:T(1,128)} %reshape.171), calls=%async_computation.2 | async-start | bytes 8192 | tf_op jit(solution)/shard_map/all_to_all | solution.py:93
  105.1 0.3 fusion.14
  105.4 0.6 copy.26
  106.0 19.3 %reduce.1 = f32[4096,16]{1,0:T(8,128)} reduce(f32[4096,1,16]{2,1,0:T(1,128)S(1)} %bitcast.84, f32[]{:T(128)} %broadcast.132), dimensions={1}, to_apply=%bitcast.54.reduce_sub_computation | reduce | bytes 524292
  125.3 3.0 %reshape.167 = f32[8,1,8192]{2,1,0:T(1,128)} reshape(f32[4096,16]{1,0:T(8,128)} %reduce.1) | data formatting | bytes 524288
  128.3 5.0 %all-to-all-start = ((f32[8,1,8192]{2,1,0:T(1,128)}), f32[8,1,8192]{2,1,0:T(1,128)S(1)}, u32[]{:S(2)}, u32[]{:S(2)}) async-start(f32[8,1,8192]{2,1,0:T(1,128)} %reshape.167), calls=%async_computation | async-start | bytes 524288 | tf_op jit(solution)/shard_map/all_to_all | solution.py:91
  133.8 0.6 reduce.6
  134.5 0.6 reduce.4
  135.5 7.5 %all-to-all-done = f32[8,1,8192]{2,1,0:T(1,128)S(1)} async-done(((f32[8,1,8192]{2,1,0:T(1,128)}), f32[8,1,8192]{2,1,0:T(1,128)S(1)}, u32[]{:S(2)}, u32[]{:S(2)}) %all-to-all-start) | async-done | bytes 262176 | tf_op jit(solution)/shard_map/all_to_all | solution.py:91
  143.1 1.2 reduce.2
  144.3 3.9 %reshape.168 = f32[4096,1,16]{2,1,0:T(1,128)S(1)} reshape(f32[8,8192]{1,0:T(8,128)S(1)} %reduce.2) | data formatting | bytes 524288
  149.0 3.4 %convolution_bitcast_fusion = f32[1,16,2880]{2,1,0:T(8,128)} fusion(bf16[512,2880]{0,1:T(8,128)(2,1)} %all-gather.2.cloned.1.call-done, bf16[16,512]{1,0:T(8,128)(2,1)S(1)} %reshape.153, pred[16]{0:T(512)(128)(4,1)S(1)} %iota_compare_fusion.1), kind=kOutput, calls=%fused_computation.22 | convolution fusion | flops 47194112 | bytes 3149840 | tf_op jit(solution)/shard_map/dot_general | solution.py:120
  152.4 53.6 %all-reduce.2.cloned.1.call-done = f32[1,16,2880]{2,1,0:T(8,128)} async-done(((f32[1,16,2880]{2,1,0:T(8,128)}), f32[1,16,2880]{2,1,0:T(8,128)}) %all-reduce.2.cloned.1.call-update) | async-done | bytes 184336 | tf_op jit(solution)/shard_map/psum | solution.py:125
  206.0 1.6 copy.58
  (169 shorter events, 13.5 us)
Async XLA Ops:
  6.5 142.4 %all-gather.2.cloned.1.call-start = ((), (), s32[]{:S(2)}) async-start(), calls=%async_computation.3 | async-start | bytes 3686400 | tf_op jit(solution)/shard_map/all_gather | solution.py:122
  23.9 72.3 %copy-start.1 = (bf16[1,16,1024]{2,1,0:T(8,128)(2,1)S(1)}, bf16[1,16,1024]{2,1,0:T(8,128)(2,1)}, u32[]{:S(2)}) copy-start(bf16[1,16,1024]{2,1,0:T(8,128)(2,1)} %param.14) | copy-start | bytes 98308
  23.9 72.3 %copy-start = (bf16[1,16,512]{2,1,0:T(8,128)(2,1)S(1)}, bf16[1,16,512]{2,1,0:T(8,128)(2,1)}, u32[]{:S(2)}) copy-start(bf16[1,16,512]{2,1,0:T(8,128)(2,1)} %param.12) | copy-start | bytes 49156
  91.6 10.2 %all-to-all-start.1 = ((f32[8,1,128]{2,1,0:T(1,128)}), f32[8,1,128]{2,1,0:T(1,128)S(1)}, u32[]{:S(2)}, u32[]{:S(2)}) async-start(f32[8,1,128]{2,1,0:T(1,128)} %reshape.169), calls=%async_computation.1 | async-start | bytes 8192 | tf_op jit(solution)/shard_map/all_to_all | solution.py:92
  101.8 26.5 %all-to-all-start.2 = ((f32[8,1,128]{2,1,0:T(1,128)}), f32[8,1,128]{2,1,0:T(1,128)S(1)}, u32[]{:S(2)}, u32[]{:S(2)}) async-start(f32[8,1,128]{2,1,0:T(1,128)} %reshape.171), calls=%async_computation.2 | async-start | bytes 8192 | tf_op jit(solution)/shard_map/all_to_all | solution.py:93
  128.3 14.7 %all-to-all-start = ((f32[8,1,8192]{2,1,0:T(1,128)}), f32[8,1,8192]{2,1,0:T(1,128)S(1)}, u32[]{:S(2)}, u32[]{:S(2)}) async-start(f32[8,1,8192]{2,1,0:T(1,128)} %reshape.167), calls=%async_computation | async-start | bytes 524288 | tf_op jit(solution)/shard_map/all_to_all | solution.py:91
  133.4 72.6 %all-reduce.2.cloned.1.call-start = ((), (), s32[]{:S(2)}) async-start(), calls=%async_computation.4 | async-start | bytes 376832 | tf_op jit(solution)/shard_map/psum | solution.py:125
Sparse Core Ops, SparseCore 0:
  9.2 44.9 all-gather.1
  152.5 53.4 all-reduce.1
where the time goes:
time: 216 us; the launch traced here: 214 us
  waiting for transfers between devices  65.8 us (30%)
  local copies, waits for them, and re-layouts  53.4 us (25%)
  other arithmetic  42.9 us (20%)
  blocking collectives  15.9 us (7%)
  between operations  14.3 us (7%)
  starting transfers between devices  13.2 us (6%)
  matrix products  8.29 us (4%)
    psum x1, waiting for transfers between devices, local(): mixed = lax.psum(projected, 'tp')  53.6 us
    gather x8, local copies, waits for them, and re-layouts, local_block(): kv_pages[block_ids]  32.4 us
    unnamed x3, other arithmetic  20.7 us
    all_gather x1, blocking collectives, local(): gathered = lax.all_gather(queries, 'tp', axis=2, tiled=True)[0]  15.9 us
    select_n x8, other arithmetic, local_block(): block_lengths = jnp.where(block_slots < live_count, block_lengths, 0)  11 us
    unnamed x12, local copies, waits for them, and re-layouts  10.6 us
    all_to_all x1, waiting for transfers between devices, local(): lax.all_to_all(weighted[None], 'tp', split_axis=2, concat_axis=0, tiled=T...  7.53 us
    select_n x8, other arithmetic, local_block(): kv_pages[block_ids]  5.57 us
  transfers between devices with their start and end apart: 5, of which 3 were waited for; matrix products, arithmetic and copies ran while one was open for 46% of the time, Pallas kernels for 0%

commit v1 on v0

--- a/solution.py
+++ b/solution.py
@@ -122,7 +122,7 @@
         lax.all_gather(out_weight, "grp", axis=1, tiled=True),
         preferred_element_type=jnp.float32,
     )
-    mixed = lax.psum(projected, "tp")
+    mixed = jnp.sum(lax.all_gather(projected, "tp"), axis=0)
     return mixed[None]
 
 

time: 216 us -> 186 us (0.86)
  waiting for transfers between devices: 65.8 us -> 36.1 us
    psum x1 -> x0, waiting for transfers between devices: 53.6 us -> none  [local(): mixed = lax.psum(projected, 'tp')]
    all_gather x0 -> x1, waiting for transfers between devices: none -> 23.9 us  [local(): mixed = jnp.sum(lax.all_gather(projected, 'tp'), axis=0)]
    unnamed x12 -> x11, local copies, waits for them, and re-layouts: 10.6 us -> 9.02 us
  transfers between devices with their start and end apart: 5 -> 5, of which waited for: 3 -> 3; matrix products, arithmetic and copies ran while one was open for 46% -> 54% of each run, Pallas kernels for 0% -> 0%
where the time goes in v1:
time: 186 us; the launch traced here: 185 us
  local copies, waits for them, and re-layouts  51.8 us (28%)
  other arithmetic  45 us (24%)
  waiting for transfers between devices  36.1 us (19%)
  blocking collectives  15.9 us (9%)
  between operations  14.3 us (8%)
  starting transfers between devices  13.2 us (7%)
  matrix products  8.29 us (4%)
    gather x8, local copies, waits for them, and re-layouts, local_block(): kv_pages[block_ids]  32.4 us
    all_gather x1, waiting for transfers between devices, local(): mixed = jnp.sum(lax.all_gather(projected, 'tp'), axis=0)  23.9 us
    unnamed x3, other arithmetic  20.7 us
    all_gather x1, blocking collectives, local(): gathered = lax.all_gather(queries, 'tp', axis=2, tiled=True)[0]  15.9 us
    select_n x8, other arithmetic, local_block(): block_lengths = jnp.where(block_slots < live_count, block_lengths, 0)  11 us
    unnamed x11, local copies, waits for them, and re-layouts  9.02 us
    all_to_all x1, waiting for transfers between devices, local(): lax.all_to_all(weighted[None], 'tp', split_axis=2, concat_axis=0, tiled=T...  7.53 us
    select_n x8, other arithmetic, local_block(): kv_pages[block_ids]  5.57 us
  transfers between devices with their start and end apart: 5, of which 3 were waited for; matrix products, arithmetic and copies ran while one was open for 54% of the time, Pallas kernels for 0%

profile of v1, /device:TPU:0, one launch (start us, length us, event | category | flops | bytes accessed | tf_op | source)
XLA Modules:
  0.0 185.3 jit_solution(13147229185468539076)
XLA Ops:
  6.5 0.7 all-gather.4.cloned.1.call-update
  7.9 15.9 %all_gather.12 = bf16[1,16,4096]{2,1,0:T(8,128)(2,1)S(1)} all-gather(bf16[1,16,512]{2,1,0:T(8,128)(2,1)} %param.12), channel_id=1, replica_groups=mesh['grp'=4,'tp'=8] {'tp'}, dimensions={2}, use_global_device_ids=true | all-gather | bytes 147456 | tf_op jit(solution)/shard_map/all_gather | solution.py:54
  23.9 65.7 %while.14 = (s32[]{:T(128)}, f32[16,4096]{1,0:T(8,128)S(1)}, f32[16,64]{1,0:T(8,128)S(1)}, f32[16,64]{1,0:T(8,128)S(1)}, s32[]{:T(128)}, /*index=5*/s32[]{:T(128...) while((s32[]{:T(128)}, f32[16,4096]{1,0:T(8,128)S(1)}, ...), condition=%wide.region_3.4_spmd, body=%wide.region_0.3_spmd.sunk | while | flops 8685212 | bytes 7998579 | solution.py:87
  24.0 1.4 compare_select_fusion.8
  25.6 0.7 compare_select_fusion.7
  26.4 4.0 %gather_fusion = bf16[32,16,1024]{2,1,0:T(8,128)(2,1)S(1)} fusion(bf16[256,16,1024]{2,1,0:T(8,128)(2,1)} %get-tuple-element.223, s32[1024]{0:T(1024)S(1)} %pad_clamp_fusion.2), kind=kCustom, calls=%fused_computation.clone.1 | custom fusion | bytes 2097280 | tf_op jit(solution)/shard_map/while/body/gather | solution.py:72
  30.8 0.3 fusion.50
  31.6 0.3 fusion.51
  32.1 1.4 compare_select_fusion.8
  33.7 0.7 compare_select_fusion.7
  34.5 4.5 %gather_fusion = bf16[32,16,1024]{2,1,0:T(8,128)(2,1)S(1)} fusion(bf16[256,16,1024]{2,1,0:T(8,128)(2,1)} %get-tuple-element.223, s32[1024]{0:T(1024)S(1)} %pad_clamp_fusion.2), kind=kCustom, calls=%fused_computation.clone.1 | custom fusion | bytes 2097280 | tf_op jit(solution)/shard_map/while/body/gather | solution.py:72
  39.5 0.3 fusion.50
  40.3 0.3 fusion.51
  40.7 1.4 compare_select_fusion.8
  42.4 0.7 compare_select_fusion.7
  43.2 4.0 %gather_fusion = bf16[32,16,1024]{2,1,0:T(8,128)(2,1)S(1)} fusion(bf16[256,16,1024]{2,1,0:T(8,128)(2,1)} %get-tuple-element.223, s32[1024]{0:T(1024)S(1)} %pad_clamp_fusion.2), kind=kCustom, calls=%fused_computation.clone.1 | custom fusion | bytes 2097280 | tf_op jit(solution)/shard_map/while/body/gather | solution.py:72
  47.6 0.3 fusion.50
  48.4 0.3 fusion.51
  48.9 1.4 compare_select_fusion.8
  50.5 0.7 compare_select_fusion.7
  51.3 4.0 %gather_fusion = bf16[32,16,1024]{2,1,0:T(8,128)(2,1)S(1)} fusion(bf16[256,16,1024]{2,1,0:T(8,128)(2,1)} %get-tuple-element.223, s32[1024]{0:T(1024)S(1)} %pad_clamp_fusion.2), kind=kCustom, calls=%fused_computation.clone.1 | custom fusion | bytes 2097280 | tf_op jit(solution)/shard_map/while/body/gather | solution.py:72
  55.7 0.3 fusion.50
  56.6 0.3 fusion.51
  57.0 1.4 compare_select_fusion.8
  58.7 0.7 compare_select_fusion.7
  59.4 4.0 %gather_fusion = bf16[32,16,1024]{2,1,0:T(8,128)(2,1)S(1)} fusion(bf16[256,16,1024]{2,1,0:T(8,128)(2,1)} %get-tuple-element.223, s32[1024]{0:T(1024)S(1)} %pad_clamp_fusion.2), kind=kCustom, calls=%fused_computation.clone.1 | custom fusion | bytes 2097280 | tf_op jit(solution)/shard_map/while/body/gather | solution.py:72
  63.9 0.3 fusion.50
  64.7 0.3 fusion.51
  65.2 1.4 compare_select_fusion.8
  66.8 0.7 compare_select_fusion.7
  67.6 4.0 %gather_fusion = bf16[32,16,1024]{2,1,0:T(8,128)(2,1)S(1)} fusion(bf16[256,16,1024]{2,1,0:T(8,128)(2,1)} %get-tuple-element.223, s32[1024]{0:T(1024)S(1)} %pad_clamp_fusion.2), kind=kCustom, calls=%fused_computation.clone.1 | custom fusion | bytes 2097280 | tf_op jit(solution)/shard_map/while/body/gather | solution.py:72
  72.0 0.3 fusion.50
  72.9 0.3 fusion.51
  73.3 1.4 compare_select_fusion.8
  74.9 0.7 compare_select_fusion.7
  75.7 4.0 %gather_fusion = bf16[32,16,1024]{2,1,0:T(8,128)(2,1)S(1)} fusion(bf16[256,16,1024]{2,1,0:T(8,128)(2,1)} %get-tuple-element.223, s32[1024]{0:T(1024)S(1)} %pad_clamp_fusion.2), kind=kCustom, calls=%fused_computation.clone.1 | custom fusion | bytes 2097280 | tf_op jit(solution)/shard_map/while/body/gather | solution.py:72
  80.2 0.3 fusion.50
  81.0 0.3 fusion.51
  81.5 1.4 compare_select_fusion.8
  83.1 0.7 compare_select_fusion.7
  83.9 4.0 %gather_fusion = bf16[32,16,1024]{2,1,0:T(8,128)(2,1)S(1)} fusion(bf16[256,16,1024]{2,1,0:T(8,128)(2,1)} %get-tuple-element.223, s32[1024]{0:T(1024)S(1)} %pad_clamp_fusion.2), kind=kCustom, calls=%fused_computation.clone.1 | custom fusion | bytes 2097280 | tf_op jit(solution)/shard_map/while/body/gather | solution.py:72
  88.3 0.3 fusion.50
  89.1 0.3 fusion.51
  89.7 0.5 broadcast.132
  90.2 0.7 reduce.5
  90.9 0.7 reshape.170
  91.6 4.6 %all-to-all-start.1 = ((f32[8,1,128]{2,1,0:T(1,128)}), f32[8,1,128]{2,1,0:T(1,128)S(1)}, u32[]{:S(2)}, u32[]{:S(2)}) async-start(f32[8,1,128]{2,1,0:T(1,128)} %reshape.170), calls=%async_computation.1 | async-start | bytes 8192 | tf_op jit(solution)/shard_map/all_to_all | solution.py:92
  96.4 0.7 reduce.3
  97.1 0.7 reshape.172
  97.9 3.9 %all-to-all-done.1 = f32[8,1,128]{2,1,0:T(1,128)S(1)} async-done(((f32[8,1,128]{2,1,0:T(1,128)}), f32[8,1,128]{2,1,0:T(1,128)S(1)}, u32[]{:S(2)}, u32[]{:S(2)}) %all-to-all-start.1) | async-done | bytes 4128 | tf_op jit(solution)/shard_map/all_to_all | solution.py:92
  101.8 3.3 %all-to-all-start.2 = ((f32[8,1,128]{2,1,0:T(1,128)}), f32[8,1,128]{2,1,0:T(1,128)S(1)}, u32[]{:S(2)}, u32[]{:S(2)}) async-start(f32[8,1,128]{2,1,0:T(1,128)} %reshape.172), calls=%async_computation.2 | async-start | bytes 8192 | tf_op jit(solution)/shard_map/all_to_all | solution.py:93
  105.1 0.3 fusion.14
  105.4 0.6 copy.26
  106.0 19.3 %reduce.1 = f32[4096,16]{1,0:T(8,128)} reduce(f32[4096,1,16]{2,1,0:T(1,128)S(1)} %bitcast.84, f32[]{:T(128)} %broadcast.132), dimensions={1}, to_apply=%bitcast.54.reduce_sub_computation | reduce | bytes 524292
  125.3 3.0 %reshape.168 = f32[8,1,8192]{2,1,0:T(1,128)} reshape(f32[4096,16]{1,0:T(8,128)} %reduce.1) | data formatting | bytes 524288
  128.3 5.0 %all-to-all-start = ((f32[8,1,8192]{2,1,0:T(1,128)}), f32[8,1,8192]{2,1,0:T(1,128)S(1)}, u32[]{:S(2)}, u32[]{:S(2)}) async-start(f32[8,1,8192]{2,1,0:T(1,128)} %reshape.168), calls=%async_computation | async-start | bytes 524288 | tf_op jit(solution)/shard_map/all_to_all | solution.py:91
  133.8 0.6 reduce.6
  134.5 0.6 reduce.4
  135.5 7.5 %all-to-all-done = f32[8,1,8192]{2,1,0:T(1,128)S(1)} async-done(((f32[8,1,8192]{2,1,0:T(1,128)}), f32[8,1,8192]{2,1,0:T(1,128)S(1)}, u32[]{:S(2)}, u32[]{:S(2)}) %all-to-all-start) | async-done | bytes 262176 | tf_op jit(solution)/shard_map/all_to_all | solution.py:91
  143.1 1.2 reduce.2
  144.3 3.9 %reshape.169 = f32[4096,1,16]{2,1,0:T(1,128)S(1)} reshape(f32[8,8192]{1,0:T(8,128)S(1)} %reduce.2) | data formatting | bytes 524288
  148.9 3.4 %fusion.15 = f32[16,2880]{1,0:T(8,128)} fusion(bf16[512,2880]{0,1:T(8,128)(2,1)} %all-gather.4.cloned.1.call-done, bf16[16,512]{1,0:T(8,128)(2,1)S(1)} %reshape.153, pred[16]{0:T(512)(128)(4,1)S(1)} %iota_compare_fusion.1), kind=kOutput, calls=%fused_computation.34 | convolution fusion | flops 47194112 | bytes 3149840 | tf_op jit(solution)/shard_map/dot_general | solution.py:120
  152.4 23.9 %all-gather.6.cloned.1.call-done = f32[128,2880]{1,0:T(8,128)} async-done(((f32[16,2880]{1,0:T(8,128)}), f32[128,2880]{1,0:T(8,128)}) %all-gather.6.cloned.1.call-update) | async-done | bytes 1474576 | tf_op jit(solution)/shard_map/all_gather | solution.py:125
  176.3 2.1 %reduce_sum.48 = f32[16,2880]{1,0:T(8,128)} reduce(f32[8,16,2880]{2,1,0:T(8,128)} %bitcast.86, f32[]{:T(128)} %constant.58.clone.1), dimensions={0}, to_apply=%region_8.9 | reduce | flops 322560 | bytes 1658884 | tf_op jit(solution)/shard_map/reduce_sum | solution.py:125
  (169 shorter events, 13.5 us)
Async XLA Ops:
  6.5 142.4 %all-gather.4.cloned.1.call-start = ((), (), s32[]{:S(2)}) async-start(), calls=%async_computation.3 | async-start | bytes 3686400 | tf_op jit(solution)/shard_map/all_gather | solution.py:122
  23.9 72.3 %copy-start.1 = (bf16[1,16,1024]{2,1,0:T(8,128)(2,1)S(1)}, bf16[1,16,1024]{2,1,0:T(8,128)(2,1)}, u32[]{:S(2)}) copy-start(bf16[1,16,1024]{2,1,0:T(8,128)(2,1)} %param.14) | copy-start | bytes 98308
  23.9 72.3 %copy-start = (bf16[1,16,512]{2,1,0:T(8,128)(2,1)S(1)}, bf16[1,16,512]{2,1,0:T(8,128)(2,1)}, u32[]{:S(2)}) copy-start(bf16[1,16,512]{2,1,0:T(8,128)(2,1)} %param.12) | copy-start | bytes 49156
  91.6 10.2 %all-to-all-start.1 = ((f32[8,1,128]{2,1,0:T(1,128)}), f32[8,1,128]{2,1,0:T(1,128)S(1)}, u32[]{:S(2)}, u32[]{:S(2)}) async-start(f32[8,1,128]{2,1,0:T(1,128)} %reshape.170), calls=%async_computation.1 | async-start | bytes 8192 | tf_op jit(solution)/shard_map/all_to_all | solution.py:92
  101.8 26.5 %all-to-all-start.2 = ((f32[8,1,128]{2,1,0:T(1,128)}), f32[8,1,128]{2,1,0:T(1,128)S(1)}, u32[]{:S(2)}, u32[]{:S(2)}) async-start(f32[8,1,128]{2,1,0:T(1,128)} %reshape.172), calls=%async_computation.2 | async-start | bytes 8192 | tf_op jit(solution)/shard_map/all_to_all | solution.py:93
  128.3 14.7 %all-to-all-start = ((f32[8,1,8192]{2,1,0:T(1,128)}), f32[8,1,8192]{2,1,0:T(1,128)S(1)}, u32[]{:S(2)}, u32[]{:S(2)}) async-start(f32[8,1,8192]{2,1,0:T(1,128)} %reshape.168), calls=%async_computation | async-start | bytes 524288 | tf_op jit(solution)/shard_map/all_to_all | solution.py:91
  133.4 42.9 %all-gather.6.cloned.1.call-start = ((), (), s32[]{:S(2)}) async-start(), calls=%async_computation.4 | async-start | bytes 1695744 | tf_op jit(solution)/shard_map/all_gather | solution.py:125
Sparse Core Ops, SparseCore 0:
  9.2 44.9 all-gather.3
  152.5 23.7 all-gather.5
